TPU v7x, 256 devices: a whole 4x4x8 slice. The times are simulated.
256 devices in a mesh: dp: 16 (over z_hi, x, core), fsdp: 16 (over z_lo, y).
Axes of the slice: x: 4, y: 4, z: 8 (z_hi: 2, z_lo: 4; z = z_hi * 4 + z_lo), core: 2. Of those that a mesh axis runs over, the one named last changes fastest.
Arguments:
- attn_heads: bfloat16 [512, 4096], P('dp', 'fsdp'), may hold values from -6 to 6
- out_proj: bfloat16 [4096, 4608], P('fsdp'), may hold values from -0.09375 to 0.09375
- resid_pre: bfloat16 [512, 4608], P(('dp', 'fsdp')), may hold values from -25 to 25
- post_gain: float32 [4608], replicated, may hold values from 0.5 to 1.5
- enc_weight: bfloat16 [4608, 65536], P(None, ('dp', 'fsdp')), may hold values from -0.09375 to 0.09375
- enc_bias: float32 [65536], P(('dp', 'fsdp')), may hold values from -3 to 3
- dec_weight: bfloat16 [65536, 4608], P(('dp', 'fsdp')), may hold values from -0.046875 to 0.046875
- dec_bias: float32 [4608], replicated, may hold values from -3 to 3
Outputs:
- enc_grad: bfloat16 [4608, 65536], P(None, ('dp', 'fsdp'))
- enc_bias_grad: float32 [65536], P(('dp', 'fsdp'))
- dec_grad: bfloat16 [65536, 4608], P(('dp', 'fsdp'))
- dec_bias_grad: float32 [4608], replicated
- loss: float32 [], replicated
All inputs are finite; a program needn't handle non-finite values.
Results may differ from a plain program's by a relative error of at most 0.013.
Values may be sent and summed in bfloat16 or wider, within the bound.
A program may use at most 128 MiB of HBM per device.

v0:
```python
import jax
import jax.numpy as jnp
from jax import lax
from jax.sharding import PartitionSpec as P

SPARSITY = 0.25
SMOOTHING = 0.1
EPSILON = 1e-06


def finish(summed, resid_rows, post_gain):
    scale = lax.rsqrt(jnp.mean(summed * summed, axis=-1, keepdims=True) + EPSILON)
    return (resid_rows.astype(jnp.float32) + summed * scale * post_gain).astype(jnp.bfloat16)


def body(attn_heads, out_proj, resid_pre, post_gain, enc_weight, enc_bias, dec_weight, dec_bias):
    block = attn_heads
    summed = lax.psum_scatter(
        jnp.dot(block, out_proj, preferred_element_type=jnp.float32),
        "fsdp",
        scatter_dimension=0,
        tiled=True,
    )
    resid_own = finish(summed, resid_pre, post_gain)
    resid_all = lax.all_gather(resid_own, ("dp", "fsdp"), axis=0, tiled=True)
    preact = jnp.dot(resid_all, enc_weight, preferred_element_type=jnp.float32) + enc_bias
    latents = jnp.maximum(preact, 0.0)
    latents_b = latents.astype(jnp.bfloat16)
    row_norms = jnp.sqrt(jnp.sum(jnp.square(dec_weight.astype(jnp.float32)), axis=1) + EPSILON)
    penalty_local = jnp.sum(latents * row_norms)
    penalty_total = lax.psum(penalty_local, ("dp", "fsdp"))
    block = latents_b
    recon = lax.psum_scatter(
        jnp.dot(block, dec_weight, preferred_element_type=jnp.float32),
        ("dp", "fsdp"),
        scatter_dimension=0,
        tiled=True,
    )
    recon = recon + dec_bias
    error = recon - resid_own.astype(jnp.float32)
    error_local = jnp.sum(error * error)
    error_total = lax.psum(error_local, ("dp", "fsdp"))
    loss = (0.5 * error_total + SPARSITY * penalty_total) / (
        resid_all.shape[0] * resid_all.shape[1]
    )
    error_b = error.astype(jnp.bfloat16)
    error_all = lax.all_gather(error_b, ("dp", "fsdp"), axis=0, tiled=True)
    dec_bias_grad = jnp.sum(error_all, axis=0, dtype=jnp.float32)
    usage = jnp.sum(latents, axis=0)
    dec_grad = lax.dot_general(
        latents_b, error_all, (((0,), (0,)), ((), ())), preferred_element_type=jnp.float32
    )
    dec_grad = (
        dec_grad + SPARSITY * (usage / row_norms)[:, None] * dec_weight.astype(jnp.float32)
    ).astype(jnp.bfloat16)
    latent_grad = lax.dot_general(
        error_all, dec_weight, (((1,), (1,)), ((), ())), preferred_element_type=jnp.float32
    )
    latent_grad = latent_grad + SPARSITY * row_norms
    preact_grad = latent_grad * jax.nn.sigmoid(preact / SMOOTHING)
    enc_bias_grad = jnp.sum(preact_grad, axis=0)
    enc_grad = lax.dot_general(
        resid_all,
        preact_grad.astype(jnp.bfloat16),
        (((0,), (0,)), ((), ())),
        preferred_element_type=jnp.float32,
    ).astype(jnp.bfloat16)
    return (enc_grad, enc_bias_grad, dec_grad, dec_bias_grad, loss)


def solution(mesh):
    placed = (
        P("dp", "fsdp"),
        P("fsdp", None),
        P(("dp", "fsdp"), None),
        P(),
        P(None, ("dp", "fsdp")),
        P(("dp", "fsdp")),
        P(("dp", "fsdp"), None),
        P(),
    )
    return jax.shard_map(
        body,
        mesh=mesh,
        in_specs=placed,
        out_specs=(P(None, ("dp", "fsdp")), P(("dp", "fsdp")), P(("dp", "fsdp"), None), P(), P()),
        check_vma=False,
    )
```

profile of v0, /device:TPU:1, one launch (start us, length us, event | category | flops | bytes accessed | tf_op | source)
XLA Modules:
  0.0 1924.5 jit_solution(9511033964533940527)
XLA Ops:
  7.2 0.0 all-reduce.6.cloned.1.call-start
  7.2 1.6 copy-done
  8.8 2.0 fusion.9
  10.9 0.0 all-gather.5.cloned.1.call-start
  11.0 1.3 dynamic-slice
  12.9 153.1 %all-reduce.6.cloned.1.call-done = f32[32,4608]{1,0:T(8,128)} async-done(((f32[32,4608]{1,0:T(8,128)}), f32[32,4608]{1,0:T(8,128)}) %all-reduce.6.cloned.1.call-update) | async-done | bytes 589840
  166.0 1.1 multiply_reduce_fusion.2
  167.1 1.6 add_convert_fusion
  168.7 0.0 all-reduce.8.cloned.1.call-start
  168.8 2.2 fusion.1
  171.0 716.5 %all-gather.5.cloned.1.call-done = bf16[256,2,4608]{2,1,0:T(2,128)(2,1)} async-done(((bf16[1,2,4608]{2,1,0:T(2,128)(2,1)}), bf16[256,2,4608]{2,1,0:T(2,128)(2,1)}) %all-gather.5.cloned.1.call-update) | async-done | bytes 4718608 | tf_op jit(solution)/shard_map/all_gather | solution.py:25
  887.5 7.6 reshape.38
  895.1 5.2 multiply_reduce_fusion
  900.3 5.1 fusion.4
  905.4 0.0 all-gather.7.cloned.1.call-start
  905.4 277.4 %all-reduce.8.cloned.1.call-done = f32[512,4608]{1,0:T(8,128)} async-done(((f32[512,4608]{1,0:T(8,128)}), f32[512,4608]{1,0:T(8,128)}) %all-reduce.8.cloned.1.call-update) | async-done | bytes 9437200
  1182.8 2.2 multiply_reduce_fusion.1
  1185.0 77.7 %all-reduce.2 = (f32[]{:T(128)}, f32[]{:T(128)}) all-reduce(f32[]{:T(128)} %get-tuple-element.9, f32[]{:T(128)} %get-tuple-element.5), channel_id=1, replica_groups=mesh['dp'=16,'fsdp'=16] {'dp','fsdp'}, use_global_device_ids=true, to_apply=%region_8.0 | all-reduce | flops 2 | bytes 16 | tf_op jit(solution)/shard_map/psum | solution.py:42
  1264.0 631.6 %all-gather.7.cloned.1.call-done = bf16[256,2,4608]{2,1,0:T(2,128)(2,1)} async-done(((bf16[1,2,4608]{2,1,0:T(2,128)(2,1)}), bf16[256,2,4608]{2,1,0:T(2,128)(2,1)}) %all-gather.7.cloned.1.call-update) | async-done | bytes 4718608 | tf_op jit(solution)/shard_map/all_gather | solution.py:47
  1895.6 7.6 reshape.40
  1903.2 4.1 convert_reduce_fusion
  1907.3 3.8 fusion.8
  1911.1 2.9 fusion
  1914.0 2.9 convolution_convert_fusion
  (25 shorter events, 0.1 us)
Async XLA Ops:
  7.2 1.7 copy-start
  7.2 158.8 %all-reduce.6.cloned.1.call-start = ((), (), s32[]{:S(2)}) async-start(), calls=%async_computation.2 | async-start | bytes 1179648
  10.9 876.6 %all-gather.5.cloned.1.call-start = ((), (), s32[]{:S(2)}) async-start(), calls=%async_computation | async-start | bytes 4737024 | tf_op jit(solution)/shard_map/all_gather | solution.py:25
  168.7 1014.1 %all-reduce.8.cloned.1.call-start = ((), (), s32[]{:S(2)}) async-start(), calls=%async_computation.3 | async-start | bytes 18874368
  171.0 724.0 %copy-start.6 = (f32[256]{0:T(256)S(1)}, f32[256]{0:T(256)}, u32[]{:S(2)}) copy-start(f32[256]{0:T(256)} %param.13) | copy-start | bytes 3076
  895.0 5.2 copy-start.2
  905.3 277.5 %copy-start.4 = (bf16[2,4608]{1,0:T(2,128)(2,1)S(1)}, bf16[2,4608]{1,0:T(2,128)(2,1)}, u32[]{:S(2)}) copy-start(bf16[2,4608]{1,0:T(2,128)(2,1)} %add_convert_fusion) | copy-start | bytes 55300
  905.3 277.5 %copy-start.5 = (f32[4608]{0:T(1024)S(1)}, f32[4608]{0:T(1024)}, u32[]{:S(2)}) copy-start(f32[4608]{0:T(1024)} %param.15) | copy-start | bytes 55300
  905.4 990.3 %all-gather.7.cloned.1.call-start = ((), (), s32[]{:S(2)}) async-start(), calls=%async_computation.1 | async-start | bytes 4737024 | tf_op jit(solution)/shard_map/all_gather | solution.py:47
  1903.2 4.1 copy-start.1
  1903.2 10.7 slice-start
  1907.3 3.8 copy-start.3
  1907.3 6.7 slice-start.1
Sparse Core Ops, SparseCore 0:
  11.2 154.7 all-reduce.5
  168.8 718.5 all-gather.4
  905.5 277.2 all-reduce.7
  1185.1 710.4 all-gather.6
where the time goes:
time: 1930 us; the launch traced here: 1920 us
  waiting for transfers between devices  1780 us (92%)
  blocking collectives  77.7 us (4%)
  matrix products  21.8 us (1%)
    all_gather x1, waiting for transfers between devices, body(): resid_all = lax.all_gather(resid_own, ('dp', 'fsdp'), axis=0, tiled=True)  716 us
    all_gather x1, waiting for transfers between devices, body(): error_all = lax.all_gather(error_b, ('dp', 'fsdp'), axis=0, tiled=True)  632 us
    unnamed x6, waiting for transfers between devices  431 us
    psum x1, blocking collectives, body(): error_total = lax.psum(error_local, ('dp', 'fsdp'))  77.7 us
  transfers between devices with their start and end apart: 4, of which 4 were waited for; matrix products, arithmetic and copies ran while one was open for 0% of the time, Pallas kernels for 0%

commit v1 on v0

v1 whole, which is shorter than its diff:
```python
import jax
import jax.numpy as jnp
from jax import lax
from jax.experimental import pallas as pl
from jax.experimental.pallas import tpu as pltpu
from jax.sharding import PartitionSpec as P

SPARSITY = 0.25
SMOOTHING = 0.1
EPSILON = 1e-06

D = 4608
BLOCKS = 64
MESH = pl.DeviceIdType.MESH


def coords():
    dp, fs = lax.axis_index("dp"), lax.axis_index("fsdp")
    x = lax.rem(lax.div(dp, 2), 4)
    y = lax.rem(fs, 4)
    z = lax.div(dp, 8) * 4 + lax.div(fs, 4)
    return x, y, z, lax.rem(dp, 2)


def device(x, y, z, c):
    return ((lax.div(z, 4) * 4 + x) * 2 + c, lax.rem(z, 4) * 4 + y)


class Wire:
    def __init__(self, send_sems, recv_sems):
        self.send_sems, self.recv_sems, self.copies = send_sems, recv_sems, []

    def send(self, src, dst, target):
        n = len(self.copies)
        copy = pltpu.make_async_remote_copy(
            src_ref=src,
            dst_ref=dst,
            send_sem=self.send_sems.at[n],
            recv_sem=self.recv_sems.at[n],
            device_id=target,
            device_id_type=MESH,
        )
        copy.start()
        self.copies.append(copy)
        return copy

    def finish(self):
        for copy in self.copies:
            copy.wait_send()


def arrived(copies):
    for copy in copies:
        copy.wait_recv()


def cols(start, size):
    return pl.ds(pl.multiple_of(start, 128), size)


def greet(targets):
    barrier = pltpu.get_barrier_semaphore()
    for target in targets:
        pl.semaphore_signal(barrier, inc=1, device_id=target, device_id_type=MESH)
    pl.semaphore_wait(barrier, len(targets))


A1 = 2048
Q1 = (D - A1) // 4
W1 = D // 4


def residual_kernel(part, pre, gain, out, rs, rp, rows, full, send_sems, recv_sems):
    x, y, z, c = coords()
    zh, zl = lax.div(z, 4) * 4, lax.rem(z, 4)
    at_x = lambda d: device(lax.rem(x + d, 4), y, z, c)
    at_y = lambda d: device(x, lax.rem(y + d, 4), z, c)
    at_z = lambda d: device(x, y, lax.rem(z + d, 8), c)
    sibling = device(x, y, z, 1 - c)
    plane = {
        (a, b): device(x, lax.rem(y + a, 4), zh + lax.rem(zl + b, 4), c)
        for a in range(4)
        for b in range(4)
        if (a, b) != (0, 0)
    }
    beyond = [device(x, y, lax.rem(zl + d, 4) + 4 - zh, c) for d in range(4)]
    greet(
        list(plane.values())
        + beyond
        + [at_x(d) for d in (1, 2, 3)]
        + [sibling]
    )
    wire = Wire(send_sems, recv_sems)

    got = []
    for i, ((a, b), target) in enumerate(plane.items()):
        src = part.at[lax.rem(zl + b, 4), :, cols(lax.rem(y + a, 4) * W1, W1)]
        got.append(wire.send(src, rs.at[i], target))
    rp[y] = pre[...]
    got_pre = [wire.send(rp.at[y], rp.at[y], at_y(d)) for d in (1, 2, 3)]
    total = part[zl, :, cols(y * W1, W1)].astype(jnp.float32)
    arrived(got)
    for i in range(15):
        total = total + rs[i].astype(jnp.float32)
    full[y] = total
    got = [wire.send(full.at[y], full.at[y], at_y(d)) for d in (1, 2, 3)]
    arrived(got_pre)
    for i in range(4):
        rows[2 * i : 2 * i + 2, :] = rp[i].astype(jnp.float32)
    arrived(got)
    square = jnp.zeros((8, 1), jnp.float32)
    for i in range(4):
        square = square + jnp.sum(full[i] * full[i], axis=1, keepdims=True)
    scale = lax.rsqrt(square / D + EPSILON)
    mine = c * 32 + x * 8 + z
    for i in range(4):
        w = slice(i * W1, (i + 1) * W1)
        rows[:, w] = rows[:, w] + full[i] * scale * gain[:, w]

    a_cols, q_cols = pl.ds(0, A1), cols(A1 + y * Q1, Q1)
    out[mine, :, a_cols] = rows[:, a_cols].astype(jnp.bfloat16)
    out[mine, :, q_cols] = rows[:, q_cols].astype(jnp.bfloat16)
    half = pl.ds(c * 32, 32)
    run = pl.ds(c * 32 + x * 8, 8)
    block_a, block_q = out.at[mine, :, a_cols], out.at[mine, :, q_cols]
    got_a = [wire.send(block_a, block_a, at_z(d)) for d in range(1, 8)]
    got_q = [wire.send(block_q, block_q, at_z(d)) for d in range(1, 8)]
    arrived(got_q)
    run_q = out.at[run, :, q_cols]
    got_q = [wire.send(run_q, run_q, at_x(d)) for d in (1, 2, 3)]
    arrived(got_a)
    run_a = out.at[run, :, a_cols]
    got_a = [wire.send(run_a, run_a, at_x(d)) for d in (1, 2, 3)]
    passed = [wire.send(run_a, run_a, sibling)]
    arrived(got_q)
    half_q = out.at[half, :, q_cols]
    got_q = [wire.send(half_q, half_q, at_y(d)) for d in (1, 2, 3)]
    passed.append(wire.send(half_q, half_q, sibling))
    for d in (1, 2, 3):
        got_a[d - 1].wait_recv()
        there = out.at[pl.ds(c * 32 + lax.rem(x + 4 - d, 4) * 8, 8), :, a_cols]
        passed.append(wire.send(there, there, sibling))
    for d in (1, 2, 3):
        got_q[d - 1].wait_recv()
        there = out.at[half, :, cols(A1 + lax.rem(y + 4 - d, 4) * Q1, Q1)]
        passed.append(wire.send(there, there, sibling))
    arrived(passed)
    wire.finish()


def gather_residual(part, pre, gain):
    copies = 15 + 3 + 3 + 14 + 9 + 8
    vmem = pl.BlockSpec(memory_space=pltpu.VMEM)
    return pl.pallas_call(
        residual_kernel,
        out_shape=jax.ShapeDtypeStruct((BLOCKS, 8, D), jnp.bfloat16),
        in_specs=[vmem] * 3,
        out_specs=vmem,
        scratch_shapes=[
            pltpu.VMEM((15, 8, W1), jnp.bfloat16),
            pltpu.VMEM((4, 2, D), jnp.bfloat16),
            pltpu.VMEM((8, D), jnp.float32),
            pltpu.VMEM((4, 8, W1), jnp.float32),
            pltpu.SemaphoreType.DMA((copies,)),
            pltpu.SemaphoreType.DMA((copies,)),
        ],
        compiler_params=pltpu.CompilerParams(
            collective_id=0, has_side_effects=True, vmem_limit_bytes=24 * 2**20
        ),
        name="gather_residual",
    )(part, pre, gain)


A2 = 2560
QA = A2 // 4
C2 = D - A2
QC = C2 // 4


def error_kernel(
    part, resid, bias, penalty, out, stats,
    sib, both, ra1, rc1, acc_a, acc_c, ra2, rc2, acc_a2, acc_c2, ra3, rc3, st_z, st_x, st_y, st_c,
    send_sems, recv_sems,
):
    x, y, z, c = coords()
    at_x = lambda d: device(lax.rem(x + d, 4), y, z, c)
    at_y = lambda d: device(x, lax.rem(y + d, 4), z, c)
    at_z = lambda d: device(x, y, lax.rem(z + d, 8), c)
    sibling = device(x, y, z, 1 - c)
    greet(
        [at_x(d) for d in (1, 2, 3)]
        + [at_y(d) for d in (1, 2, 3)]
        + [at_z(d) for d in range(1, 8)]
        + [sibling]
    )
    wire = Wire(send_sems, recv_sems)
    f32 = jnp.float32
    base = c * 32
    c_cols = pl.ds(A2, C2)

    order_a = (1, 2, 3, 0)
    got_a, got_c = {}, {}
    for d in order_a:
        w = cols(lax.rem(y + d, 4) * QA, QA)
        got_a[d] = wire.send(part.at[pl.ds(32 - base, 32), :, w], sib.at[:, :, w], sibling)
        r = lax.rem(x + d, 4) * 8
        got_c[d] = wire.send(
            part.at[pl.ds(32 - base + r, 8), :, c_cols], sib.at[pl.ds(r, 8), :, c_cols], sibling
        )
    from_a, from_c = {}, {}
    for d in order_a:
        w = cols(lax.rem(y + d, 4) * QA, QA)
        got_a[d].wait_recv()

        @pl.loop(0, 32)
        def _(i):
            both[i, :, w] = (part[base + i, :, w].astype(f32) + sib[i, :, w].astype(f32)).astype(jnp.bfloat16)

        if d:
            from_a[d] = wire.send(both.at[:, :, w], ra1.at[d - 1], at_y(d))
        r = lax.rem(x + d, 4) * 8
        got_c[d].wait_recv()

        @pl.loop(0, 8)
        def _(i):
            both[r + i, :, c_cols] = (
                part[base + r + i, :, c_cols].astype(f32) + sib[r + i, :, c_cols].astype(f32)
            ).astype(jnp.bfloat16)

        if d:
            from_c[d] = wire.send(both.at[pl.ds(r, 8), :, c_cols], rc1.at[d - 1], at_x(d))

    wa, wc = cols(y * QA, QA), cols(A2 + y * QC, QC)
    arrived(from_a.values())

    @pl.loop(0, 32)
    def _(i):
        acc_a[i] = (
            both[i, :, wa].astype(f32) + ra1[0, i].astype(f32) + ra1[1, i].astype(f32) + ra1[2, i].astype(f32)
        ).astype(jnp.bfloat16)

    from_a = [
        wire.send(acc_a.at[pl.ds(lax.rem(x + d, 4) * 8, 8)], ra2.at[d - 1], at_x(d)) for d in (1, 2, 3)
    ]
    arrived(from_c.values())

    @pl.loop(0, 8)
    def _(i):
        acc_c[i] = (
            both[x * 8 + i, :, c_cols].astype(f32)
            + rc1[0, i].astype(f32) + rc1[1, i].astype(f32) + rc1[2, i].astype(f32)
        ).astype(jnp.bfloat16)

    from_c = [
        wire.send(acc_c.at[:, :, cols(lax.rem(y + d, 4) * QC, QC)], rc2.at[d - 1], at_y(d))
        for d in (1, 2, 3)
    ]

    arrived(from_a)

    @pl.loop(0, 8)
    def _(i):
        acc_a2[i] = (
            acc_a[x * 8 + i].astype(f32) + ra2[0, i].astype(f32) + ra2[1, i].astype(f32) + ra2[2, i].astype(f32)
        ).astype(jnp.bfloat16)

    from_a = [wire.send(acc_a2.at[lax.rem(z + d, 8)], ra3.at[d - 1], at_z(d)) for d in range(1, 8)]
    arrived(from_c)

    @pl.loop(0, 8)
    def _(i):
        acc_c2[i] = (
            acc_c[i, :, cols(y * QC, QC)].astype(f32)
            + rc2[0, i].astype(f32) + rc2[1, i].astype(f32) + rc2[2, i].astype(f32)
        ).astype(jnp.bfloat16)

    from_c = [wire.send(acc_c2.at[lax.rem(z + d, 8)], rc3.at[d - 1], at_z(d)) for d in range(1, 8)]

    mine = base + x * 8 + z
    square = penalty[...]

    def error_of(total, w, size, square):
        error = total + bias[:, w] - resid[mine, :, w].astype(f32)
        out[mine, :, w] = error.astype(jnp.bfloat16)
        for i in range(size // 128):
            piece = error[:, i * 128 : (i + 1) * 128]
            square = square + 0.5 * piece * piece
        return square

    arrived(from_a)
    total = acc_a2[z].astype(f32)
    for i in range(7):
        total = total + ra3[i].astype(f32)
    square = error_of(total, wa, QA, square)
    block_a = out.at[mine, :, wa]
    got_a = [wire.send(block_a, block_a, at_z(d)) for d in range(1, 8)]
    arrived(from_c)
    total = acc_c2[z].astype(f32)
    for i in range(7):
        total = total + rc3[i].astype(f32)
    square = error_of(total, wc, QC, square)
    block_c = out.at[mine, :, wc]
    got_c = [wire.send(block_c, block_c, at_z(d)) for d in range(1, 8)]
    st_z[z] = square
    got_s = [wire.send(st_z.at[z], st_z.at[z], at_z(d)) for d in range(1, 8)]

    half = pl.ds(base, 32)
    run = pl.ds(base + x * 8, 8)
    arrived(got_a)
    run_a = out.at[run, :, wa]
    got_a = [wire.send(run_a, run_a, at_x(d)) for d in (1, 2, 3)]
    arrived(got_c)
    run_c = out.at[run, :, wc]
    got_c = [wire.send(run_c, run_c, at_y(d)) for d in (1, 2, 3)]
    arrived(got_s)
    st_x[x] = sum_of(st_z, 8)
    got_s = [wire.send(st_x.at[x], st_x.at[x], at_x(d)) for d in (1, 2, 3)]
    arrived(got_a)
    half_a = out.at[half, :, wa]
    got_a = [wire.send(half_a, half_a, at_y(d)) for d in (1, 2, 3)]
    passed = [wire.send(half_a, half_a, sibling)]
    arrived(got_c)
    run_c = out.at[run, :, c_cols]
    got_c = [wire.send(run_c, run_c, at_x(d)) for d in (1, 2, 3)]
    passed.append(wire.send(run_c, run_c, sibling))
    arrived(got_s)
    st_y[y] = sum_of(st_x, 4)
    got_s = [wire.send(st_y.at[y], st_y.at[y], at_y(d)) for d in (1, 2, 3)]
    arrived(got_s)
    st_c[c] = sum_of(st_y, 4)
    got_s = wire.send(st_c.at[c], st_c.at[c], sibling)
    for d in (1, 2, 3):
        got_a[d - 1].wait_recv()
        there = out.at[half, :, cols(lax.rem(y + 4 - d, 4) * QA, QA)]
        passed.append(wire.send(there, there, sibling))
        got_c[d - 1].wait_recv()
        there = out.at[pl.ds(base + lax.rem(x + 4 - d, 4) * 8, 8), :, c_cols]
        passed.append(wire.send(there, there, sibling))
    got_s.wait_recv()
    stats[...] = st_c[0] + st_c[1]
    arrived(passed)
    wire.finish()


def sum_of(ref, n):
    total = ref[0]
    for i in range(1, n):
        total = total + ref[i]
    return total


def exchange_error(part, resid, bias, penalty):
    copies = 8 + 6 + 6 + 14 + 14 + 7 + 6 + 3 + 6 + 3 + 1 + 8
    vmem = pl.BlockSpec(memory_space=pltpu.VMEM)
    bf16 = jnp.bfloat16
    return pl.pallas_call(
        error_kernel,
        out_shape=(
            jax.ShapeDtypeStruct((BLOCKS, 8, D), bf16),
            jax.ShapeDtypeStruct((8, 128), jnp.float32),
        ),
        in_specs=[vmem] * 4,
        out_specs=(vmem, vmem),
        scratch_shapes=[
            pltpu.VMEM((32, 8, D), bf16),
            pltpu.VMEM((32, 8, D), bf16),
            pltpu.VMEM((3, 32, 8, QA), bf16),
            pltpu.VMEM((3, 8, 8, C2), bf16),
            pltpu.VMEM((32, 8, QA), bf16),
            pltpu.VMEM((8, 8, C2), bf16),
            pltpu.VMEM((3, 8, 8, QA), bf16),
            pltpu.VMEM((3, 8, 8, QC), bf16),
            pltpu.VMEM((8, 8, QA), bf16),
            pltpu.VMEM((8, 8, QC), bf16),
            pltpu.VMEM((7, 8, QA), bf16),
            pltpu.VMEM((7, 8, QC), bf16),
            pltpu.VMEM((8, 8, 128), jnp.float32),
            pltpu.VMEM((4, 8, 128), jnp.float32),
            pltpu.VMEM((4, 8, 128), jnp.float32),
            pltpu.VMEM((2, 8, 128), jnp.float32),
            pltpu.SemaphoreType.DMA((copies,)),
            pltpu.SemaphoreType.DMA((copies,)),
        ],
        compiler_params=pltpu.CompilerParams(
            collective_id=1, has_side_effects=True, vmem_limit_bytes=40 * 2**20
        ),
        name="exchange_error",
    )(part, resid, bias, penalty)


def body(attn_heads, out_proj, resid_pre, post_gain, enc_weight, enc_bias, dec_weight, dec_bias):
    f32, bf16 = jnp.float32, jnp.bfloat16
    part = jnp.dot(attn_heads, out_proj, preferred_element_type=f32).astype(bf16)
    resid = gather_residual(part.reshape(4, 8, D), resid_pre, post_gain.reshape(1, D))
    resid_all = resid.reshape(512, D)
    preact = jnp.dot(resid_all, enc_weight, preferred_element_type=f32) + enc_bias
    latents = jnp.maximum(preact, 0.0)
    latents_b = latents.astype(bf16)
    row_norms = jnp.sqrt(jnp.sum(jnp.square(dec_weight.astype(f32)), axis=1) + EPSILON)
    penalty = SPARSITY * jnp.sum((latents * row_norms).reshape(64, 8, 2, 128), axis=(0, 2))
    recon = jnp.dot(latents_b, dec_weight, preferred_element_type=f32).astype(bf16)
    error, stats = exchange_error(recon.reshape(BLOCKS, 8, D), resid, dec_bias.reshape(1, D), penalty)
    loss = jnp.sum(stats) / (512 * D)
    error_all = error.reshape(512, D)
    dec_bias_grad = jnp.sum(error_all, axis=0, dtype=f32)
    usage = jnp.sum(latents, axis=0)
    dec_grad = lax.dot_general(latents_b, error_all, (((0,), (0,)), ((), ())), preferred_element_type=f32)
    dec_grad = (dec_grad + SPARSITY * (usage / row_norms)[:, None] * dec_weight.astype(f32)).astype(bf16)
    latent_grad = lax.dot_general(error_all, dec_weight, (((1,), (1,)), ((), ())), preferred_element_type=f32)
    latent_grad = latent_grad + SPARSITY * row_norms
    preact_grad = latent_grad * jax.nn.sigmoid(preact / SMOOTHING)
    enc_bias_grad = jnp.sum(preact_grad, axis=0)
    enc_grad = lax.dot_general(
        resid_all, preact_grad.astype(bf16), (((0,), (0,)), ((), ())), preferred_element_type=f32
    ).astype(bf16)
    return (enc_grad, enc_bias_grad, dec_grad, dec_bias_grad, loss)


def solution(mesh):
    placed = (
        P("dp", "fsdp"),
        P("fsdp", None),
        P(("dp", "fsdp"), None),
        P(),
        P(None, ("dp", "fsdp")),
        P(("dp", "fsdp")),
        P(("dp", "fsdp"), None),
        P(),
    )
    return jax.shard_map(
        body,
        mesh=mesh,
        in_specs=placed,
        out_specs=(P(None, ("dp", "fsdp")), P(("dp", "fsdp")), P(("dp", "fsdp"), None), P(), P()),
        check_vma=False,
    )
```

time: 1930 us -> 148 us (0.08)
  waiting for transfers between devices: 1780 us -> 0 us
  Pallas kernels: 0 us -> 118 us
  blocking collectives: 77.7 us -> 0 us
    all_gather x2 -> x0, waiting for transfers between devices: 1350 us -> none  [the longest x1 716 us: body(): resid_all = lax.all_gather(resid_own, ('dp', 'fsdp'), axis=0, tiled=True)]
    unnamed x6 -> x0, waiting for transfers between devices: 431 us -> none
    pallas_call x0 -> x2, Pallas kernels: none -> 118 us  [the longest x1 66.2 us: exchange_error(): pl.pallas_call(error_kernel, out_shape=(jax.ShapeDtypeStruct((BLOCKS, 8,...]
    psum x1 -> x0, blocking collectives: 77.7 us -> none  [body(): error_total = lax.psum(error_local, ('dp', 'fsdp'))]
  transfers between devices with their start and end apart: 4 -> 0, of which waited for: 4 -> 0; matrix products, arithmetic and copies ran while one was open for 0% -> 0% of each run, Pallas kernels for 0% -> 0%
where the time goes in v1:
time: 148 us
  Pallas kernels  118 us (80%)
  matrix products  14.2 us (10%)
  other arithmetic  7.18 us (5%)
  local copies, waits for them, and re-layouts  5.51 us (4%)
  between operations  2.57 us (2%)
    pallas_call x1, Pallas kernels, exchange_error(): pl.pallas_call(error_kernel, out_shape=(jax.ShapeDtypeStruct((BLOCKS, 8,...  66.2 us
    pallas_call x1, Pallas kernels, gather_residual(): pl.pallas_call(residual_kernel, out_shape=jax.ShapeDtypeStruct((BLOCKS, 8...  52 us
    dot_general x1, matrix products, body(): lax.dot_general(error_all, dec_weight, (((1,), (1,)), ((), ())), preferre...  4.48 us
    reduce_sum x1, other arithmetic, body(): dec_bias_grad = jnp.sum(error_all, axis=0, dtype=f32)  4.06 us
    unnamed x22, local copies, waits for them, and re-layouts  4.02 us

profile of v1, /device:TPU:1, one launch (start us, length us, event | category | flops | bytes accessed | tf_op | source)
XLA Modules:
  0.0 147.7 jit_solution(5290839280617822665)
XLA Ops:
  0.6 0.0 copy-start
  0.6 0.0 copy-start.8
  0.7 2.4 %fusion.3 = f32[256]{0:T(256)S(1)} fusion(bf16[256,4608]{1,0:T(8,128)(2,1)} %param.14), kind=kLoop, calls=%fused_computation.10 | loop fusion | flops 3538688 | bytes 2360320 | tf_op jit(solution)/shard_map/reduce_sum | solution.py:399
  3.0 0.7 reshape.49.gain
  3.8 0.7 reshape.52.bias
  4.5 1.2 fusion.2.part
  5.8 0.0 copy-done.4
  5.8 52.0 %gather_residual.1.resid = bf16[64,8,4608]{2,1,0:T(8,128)(2,1)S(1)} custom-call(bf16[4,8,4608]{2,1,0:T(8,128)(2,1)S(1)} %fusion.2.part, bf16[2,4608]{1,0:T(2,128)(2,1)S(1)} %copy-done.4, f32[1,4608]{1,0:T(1,128)S(1)} %reshape.49.gain), custom_call_target="tpu_custom_call" | custom-call | tf_op jit(solution)/shard_map/gather_residual/pallas_call | solution.py:154
  57.8 0.0 copy-start.5
  57.8 1.4 maximum_reduce_fusion
  59.2 0.1 bitcast_reduce_fusion
  59.4 1.8 %copy-done.5 = bf16[256,4608]{1,0:T(8,128)(2,1)S(1)} copy-done((bf16[256,4608]{1,0:T(8,128)(2,1)S(1)}, bf16[256,4608]{1,0:T(8,128)(2,1)}, u32[]{:S(2)}) %copy-start.5) | copy-done | bytes 2359320
  61.2 1.4 fusion.part
  62.6 66.2 %exchange_error.1 = (bf16[64,8,4608]{2,1,0:T(8,128)(2,1)S(1)}, f32[8,128]{1,0:T(8,128)S(1)}) custom-call(bf16[64,8,4608]{2,1,0:T(8,128)(2,1)S(1)} %fusion.part, bf16[64,8,4608]{2,1,0:T(8,128)(2,1)S(1)} %gather_residual.1.resid, f32[1,4608]{1,0:T(1,128)S(1)} %reshape.52.bias, f32[8,128]{1,0:T(8,128)S(1)} %broadcast_multiply_fusion.penalty), custom_call_target="tpu_custom_call" | custom-call | tf_op jit(solution)/shard_map/exchange_error/pallas_call | solution.py:356
  128.9 2.2 %copy-done.2 = bf16[64,8,4608]{2,1,0:T(8,128)(2,1)} copy-done((bf16[64,8,4608]{2,1,0:T(8,128)(2,1)}, bf16[64,8,4608]{2,1,0:T(8,128)(2,1)S(1)}, u32[]{:S(2)}) %copy-start.2) | copy-done | bytes 4718616
  131.0 0.6 reduce_sum.59
  132.3 0.0 copy-start.6
  132.3 0.0 slice-start
  132.3 4.1 %convert_reduce_fusion = f32[4608]{0:T(1024)} fusion(bf16[64,8,4608]{2,1,0:T(8,128)(2,1)} %copy-done.2), kind=kLoop, calls=%fused_computation | loop fusion | flops 4713984 | bytes 4737024 | tf_op jit(solution)/shard_map/reduce_sum | solution.py:405
  136.3 4.5 %fusion.22 = (f32[256]{0:T(256)}, bf16[512,256]{1,0:T(8,128)(2,1)S(1)}) fusion(f32[512,256]{1,0:T(8,128)S(1)} %get-tuple-element.13, f32[256]{0:T(256)S(1)} %get-tuple-element.10, bf16[256,4608]{1,0:T(8,128)(2,1)S(1)} %copy-done.6, bf16[64,8,4608]{2,1,0:T(8,128)(2,1)} %copy-done.2), kind=kOutput, calls=%fused_computation.30 | convolution fusion | flops 1209007872 | bytes 7866368 | tf_op jit(solution)/shard_map/dot_general | solution.py:409
  140.8 0.0 copy-done.3
  140.8 2.9 %fusion.1 = bf16[256,4608]{1,0:T(8,128)(2,1)} fusion(bf16[256,4608]{1,0:T(8,128)(2,1)S(1)} %copy-done.6, bf16[64,8,4608]{2,1,0:T(8,128)(2,1)S(1)} %copy-done.3, f32[256]{0:T(256)S(1)} %get-tuple-element.9, f32[512,256]{1,0:T(8,128)S(1)} %get-tuple-element.13), kind=kOutput, calls=%fused_computation.4 | convolution fusion | flops 1212940288 | bytes 9962496 | tf_op jit(solution)/shard_map/dot_general | solution.py:407
  143.7 0.0 slice-done.1
  143.7 2.9 %convolution_convert_fusion.1 = bf16[4608,256]{1,0:T(8,128)(2,1)} fusion(bf16[64,8,4608]{2,1,0:T(8,128)(2,1)S(1)} %bitcast.33, bf16[512,256]{1,0:T(8,128)(2,1)S(1)} %get-tuple-element.15), kind=kOutput, calls=%fused_computation.5 | convolution fusion | flops 1209139200 | bytes 7340032 | tf_op jit(solution)/shard_map/dot_general | solution.py:413
  (15 shorter events, 0.0 us)
Async XLA Ops:
  0.6 3.9 %copy-start = (bf16[256,4608]{1,0:T(8,128)(2,1)S(1)}, bf16[256,4608]{1,0:T(8,128)(2,1)}, u32[]{:S(2)}) copy-start(bf16[256,4608]{1,0:T(8,128)(2,1)} %param.9) | copy-start | bytes 7077892
  0.6 57.1 %copy-start.8 = (f32[256]{0:T(256)S(1)}, f32[256]{0:T(256)}, u32[]{:S(2)}) copy-start(f32[256]{0:T(256)} %param.13) | copy-start | bytes 3076
  0.7 57.1 %copy-start.7 = (bf16[4608,256]{1,0:T(8,128)(2,1)S(1)}, bf16[4608,256]{1,0:T(8,128)(2,1)}, u32[]{:S(2)}) copy-start(bf16[4608,256]{1,0:T(8,128)(2,1)} %param.12) | copy-start | bytes 7077892
  0.7 5.1 %copy-start.4 = (bf16[2,4608]{1,0:T(2,128)(2,1)S(1)}, bf16[2,4608]{1,0:T(2,128)(2,1)}, u32[]{:S(2)}) copy-start(bf16[2,4608]{1,0:T(2,128)(2,1)} %pre.1) | copy-start | bytes 55300
  57.8 4.8 %copy-start.1 = (bf16[64,8,4608]{2,1,0:T(8,128)(2,1)}, bf16[64,8,4608]{2,1,0:T(8,128)(2,1)S(1)}, u32[]{:S(2)}) copy-start(bf16[64,8,4608]{2,1,0:T(8,128)(2,1)S(1)} %gather_residual.1.resid) | copy-start | bytes 14155780
  57.8 3.4 %copy-start.5 = (bf16[256,4608]{1,0:T(8,128)(2,1)S(1)}, bf16[256,4608]{1,0:T(8,128)(2,1)}, u32[]{:S(2)}) copy-start(bf16[256,4608]{1,0:T(8,128)(2,1)} %param.14) | copy-start | bytes 7077892
  128.8 2.2 %copy-start.2 = (bf16[64,8,4608]{2,1,0:T(8,128)(2,1)}, bf16[64,8,4608]{2,1,0:T(8,128)(2,1)S(1)}, u32[]{:S(2)}) copy-start(bf16[64,8,4608]{2,1,0:T(8,128)(2,1)S(1)} %get-tuple-element.7) | copy-start | bytes 14155780
  132.3 4.1 %copy-start.6 = (bf16[256,4608]{1,0:T(8,128)(2,1)S(1)}, bf16[256,4608]{1,0:T(8,128)(2,1)}, u32[]{:S(2)}) copy-start(bf16[256,4608]{1,0:T(8,128)(2,1)} %param.14) | copy-start | bytes 7077892
  132.3 11.4 %slice-start = ((s8[4718592]{0:T(1024)(128)(4,1)}), s8[524288]{0:T(1024)(128)(4,1)S(1)}, s32[]{:S(2)}) async-start(s8[4718592]{0:T(1024)(128)(4,1)} %bitcast.32), calls=%async_computation | async-start | bytes 1048576
  136.3 4.5 %copy-start.3 = (bf16[64,8,4608]{2,1,0:T(8,128)(2,1)S(1)}, bf16[64,8,4608]{2,1,0:T(8,128)(2,1)}, u32[]{:S(2)}) copy-start(bf16[64,8,4608]{2,1,0:T(8,128)(2,1)} %copy-done.2) | copy-start | bytes 14155780
  136.3 7.4 %slice-start.1 = ((s8[4718592]{0:T(1024)(128)(4,1)}), s8[4194304]{0:T(1024)(128)(4,1)S(1)}, s32[]{:S(2)}) async-start(s8[4718592]{0:T(1024)(128)(4,1)} %bitcast.32), calls=%async_computation.1 | async-start | bytes 8388608
